TPU v7x, 128 devices: a whole 4x4x4 slice. The times are simulated.
128 devices in a mesh: row: 4 (over z), col: 16 (over x_hi, y, core), smp: 2 (over x_lo).
Axes of the slice: x: 4 (x_hi: 2, x_lo: 2; x = x_hi * 2 + x_lo), y: 4, z: 4, core: 2. Of those that a mesh axis runs over, the one named last changes fastest.
Arguments:
- pair_repr: bfloat16 [512, 512, 128], P('row', 'col'), may hold values from -6 to 6
- tri_weight: bfloat16 [128, 512], replicated, may hold values from -0.75 to 0.75
- tri_bias_weight: bfloat16 [128, 4], replicated, may hold values from -40 to 40
- tri_output_weight: bfloat16 [128, 128], replicated, may hold values from -0.5 to 0.5
- samples: bfloat16 [8, 512, 768], P('smp'), may hold values from -6 to 6
- levels: int32 [8], P('smp'), may hold values from 0 to 199
- single_cond: bfloat16 [512, 384], replicated, may hold values from -6 to 6
- noise_weight: bfloat16 [256, 384], replicated, may hold values from -0.375 to 0.375
- modulation_weight: bfloat16 [384, 1536], replicated, may hold values from -0.3125 to 0.3125
- attention_weight: bfloat16 [768, 3072], replicated, may hold values from -0.5 to 0.5
- pair_bias_weight: bfloat16 [128, 16], replicated, may hold values from -40 to 40
- output_weight: bfloat16 [768, 768], replicated, may hold values from -0.21875 to 0.21875
- output_gate_weight: bfloat16 [384, 768], replicated, may hold values from -0.3125 to 0.3125
Outputs:
- new_pair: bfloat16 [512, 512, 128], P('row', 'col')
- attn_update: bfloat16 [8, 512, 768], P('smp', ('row', 'col'))
All inputs are finite; a program needn't handle non-finite values.
Results may differ from a plain program's by a relative error of at most 0.02.
The roundings to bfloat16 on the way count: a program that leaves them out, or rounds other values in their place, can miss the bound.
Values may be sent and summed in bfloat16 or wider, within the bound.
A program may use at most 128 MiB of HBM per device.

v0:
```python
import math
import jax
import jax.numpy as jnp
from jax import lax
from jax.sharding import PartitionSpec as P

HT = 4
DT = 32
CA = 768
HD = 16
DH = 48
NE = 256
LEVELS = 200
NORM_EPSILON = 1e-05
SIGMA_DATA = 16.0
SIGMA_MAX = 160.0
SIGMA_MIN = 0.0004


def combined_all(part, axis, combine):
    gathered = jax.tree.map(lambda a: lax.all_gather(a, axis), part)

    def take(source):
        return jax.tree.map(lambda a: lax.dynamic_index_in_dim(a, source, 0, False), gathered)

    return lax.fori_loop(
        1, lax.axis_size(axis), lambda source, state: combine(state, take(source)), take(0)
    )


def normalize(values):
    values = values.astype(jnp.float32)
    average = jnp.mean(values, axis=-1, keepdims=True)
    centred = values - average
    variance = jnp.mean(centred * centred, axis=-1, keepdims=True)
    return centred * lax.rsqrt(variance + NORM_EPSILON)


def noise_features(levels):
    fraction = levels.astype(jnp.float32) / (LEVELS - 1)
    upper_root = SIGMA_MAX ** (1.0 / 7.0)
    lower_root = SIGMA_MIN ** (1.0 / 7.0)
    noise_sigma = SIGMA_DATA * (upper_root + fraction * (lower_root - upper_root)) ** 7
    scaled = 0.25 * jnp.log(noise_sigma / SIGMA_DATA)
    frequency = (
        2.0
        * math.pi
        * jnp.exp(jnp.arange(NE // 2, dtype=jnp.float32) * (math.log(100.0) / (NE // 2)))
    )
    angles = scaled[:, None] * frequency[None, :]
    return jnp.concatenate([jnp.cos(angles), jnp.sin(angles)], axis=-1)


def attend_columns(pair_cols, bias_full, tri_weight, tri_output_weight):
    row_count, col_count, channels = pair_cols.shape
    normed = normalize(pair_cols).astype(jnp.bfloat16)
    projected = jnp.dot(
        normed.reshape(row_count * col_count, channels),
        tri_weight,
        preferred_element_type=jnp.float32,
    )
    projected = projected.reshape(row_count, col_count, 4, HT * DT)
    query_part = (projected[:, :, 0] * DT ** (-0.5)).astype(jnp.bfloat16)
    key_part = projected[:, :, 1].astype(jnp.bfloat16)
    value_part = projected[:, :, 2].astype(jnp.bfloat16)
    gate_part = projected[:, :, 3]

    def one_column(column):
        query_col = lax.dynamic_index_in_dim(query_part, column, 1, keepdims=False).reshape(
            row_count, HT, DT
        )
        key_col = lax.dynamic_index_in_dim(key_part, column, 1, keepdims=False).reshape(
            row_count, HT, DT
        )
        value_col = lax.dynamic_index_in_dim(value_part, column, 1, keepdims=False).reshape(
            row_count, HT, DT
        )
        gate_col = lax.dynamic_index_in_dim(gate_part, column, 1, keepdims=False)
        scores = jnp.einsum("ihd,khd->hik", query_col, key_col, preferred_element_type=jnp.float32)
        scores = scores + bias_full
        row_peak = jnp.max(scores, axis=-1, keepdims=True)
        exponent = jnp.exp(scores - row_peak)
        row_total = jnp.sum(exponent, axis=-1)
        attended = jnp.einsum(
            "hik,khd->ihd",
            exponent.astype(jnp.bfloat16),
            value_col,
            preferred_element_type=jnp.float32,
        )
        attended = attended / jnp.transpose(row_total)[:, :, None]
        return (jax.nn.sigmoid(gate_col) * attended.reshape(row_count, HT * DT)).astype(
            jnp.bfloat16
        )

    gated = lax.map(one_column, jnp.arange(col_count, dtype=jnp.int32))
    update = jnp.einsum("jic,cz->ijz", gated, tri_output_weight, preferred_element_type=jnp.float32)
    return (pair_cols.astype(jnp.float32) + update).astype(jnp.bfloat16)


def combine_parts(first, second):
    peak_one, total_one, sum_one = first
    peak_two, total_two, sum_two = second
    row_peak = jnp.maximum(peak_one, peak_two)
    factor_one = jnp.exp(peak_one - row_peak)
    factor_two = jnp.exp(peak_two - row_peak)
    row_total = total_one * factor_one + total_two * factor_two
    sample_count, token_count, channels = sum_one.shape
    head_count = row_peak.shape[1]

    def rescale(summed, factor):
        shaped = summed.reshape(sample_count, token_count, head_count, channels // head_count)
        return (shaped * jnp.transpose(factor, (0, 2, 1))[..., None]).reshape(
            sample_count, token_count, channels
        )

    return (row_peak, row_total, rescale(sum_one, factor_one) + rescale(sum_two, factor_two))


def local(
    pair_repr,
    tri_weight,
    tri_bias_weight,
    tri_output_weight,
    samples,
    levels,
    single_cond,
    noise_weight,
    modulation_weight,
    attention_weight,
    pair_bias_weight,
    output_weight,
    output_gate_weight,
):
    rows_here, cols_here, channels = pair_repr.shape
    col_count = lax.axis_size("col")
    row_index = lax.axis_index("row")
    col_index = lax.axis_index("col")
    normed_tile = normalize(pair_repr).astype(jnp.bfloat16)
    local_bias = jnp.einsum(
        "kiz,zh->hik", normed_tile, tri_bias_weight, preferred_element_type=jnp.float32
    )
    partial_bias = lax.all_gather(local_bias, "row", axis=2, tiled=True)
    bias_full = lax.all_gather(partial_bias, "col", axis=1, tiled=True)
    columns = lax.all_to_all(pair_repr, "row", split_axis=1, concat_axis=0, tiled=True)
    updated = attend_columns(columns, bias_full, tri_weight, tri_output_weight)
    new_tile = lax.all_to_all(updated, "row", split_axis=0, concat_axis=1, tiled=True)
    sample_count = samples.shape[0]
    own_count = rows_here // col_count
    own_start = col_index * own_count
    query_start = row_index * rows_here
    key_start = col_index * cols_here
    features = noise_features(levels).astype(jnp.bfloat16)
    noise_terms = jnp.dot(features, noise_weight, preferred_element_type=jnp.float32)

    def adapt(start, count):
        trunk = lax.dynamic_slice_in_dim(single_cond, start, count, 0).astype(jnp.float32)
        conditioned = normalize(trunk[None, :, :] + noise_terms[:, None, :]).astype(jnp.bfloat16)
        activation = lax.dynamic_slice_in_dim(samples, start, count, 1)
        modulation = jnp.einsum(
            "stc,cd->std", conditioned, modulation_weight, preferred_element_type=jnp.float32
        )
        adapted = (
            jax.nn.sigmoid(modulation[..., :CA]) * normalize(activation) + modulation[..., CA:]
        ).astype(jnp.bfloat16)
        return (conditioned, adapted)

    pair_renormed = normalize(new_tile).astype(jnp.bfloat16)
    pair_bias = jnp.einsum(
        "ikz,zh->hik", pair_renormed, pair_bias_weight, preferred_element_type=jnp.float32
    )
    cond_rows, adapted_rows = adapt(query_start, rows_here)
    cond_keys, adapted_keys = adapt(key_start, cols_here)
    query_part = jnp.einsum(
        "stc,cd->std", adapted_rows, attention_weight[:, :CA], preferred_element_type=jnp.float32
    )
    query_part = (
        (query_part * DH ** (-0.5)).astype(jnp.bfloat16).reshape(sample_count, rows_here, HD, DH)
    )
    key_value = jnp.einsum(
        "stc,cd->std",
        adapted_keys,
        attention_weight[:, CA : 3 * CA],
        preferred_element_type=jnp.float32,
    )
    key_part = key_value[..., :CA].astype(jnp.bfloat16).reshape(sample_count, cols_here, HD, DH)
    value_part = key_value[..., CA:].astype(jnp.bfloat16).reshape(sample_count, cols_here, HD, DH)
    scores = (
        jnp.einsum("sihd,skhd->shik", query_part, key_part, preferred_element_type=jnp.float32)
        + pair_bias[None]
    )
    adapted_own = lax.dynamic_slice_in_dim(adapted_rows, own_start, own_count, 1)
    cond_own = lax.dynamic_slice_in_dim(cond_rows, own_start, own_count, 1)
    local_peak = jnp.max(scores, axis=-1)
    exponent = jnp.exp(scores - local_peak[..., None])
    local_total = jnp.sum(exponent, axis=-1)
    partial_value = jnp.einsum(
        "shik,skhd->sihd",
        exponent.astype(jnp.bfloat16),
        value_part,
        preferred_element_type=jnp.float32,
    )
    partial_value = partial_value.reshape(sample_count, rows_here, CA)
    row_peak, row_total, summed = combined_all(
        (local_peak, local_total, partial_value), "col", combine_parts
    )
    row_total = lax.dynamic_slice_in_dim(row_total, own_start, own_count, 2)
    summed = lax.dynamic_slice_in_dim(summed, own_start, own_count, 1)
    attended = (
        summed.reshape(sample_count, own_count, HD, DH)
        / jnp.transpose(row_total, (0, 2, 1))[..., None]
    )
    attended = attended.reshape(sample_count, own_count, CA)
    gate_part = jnp.einsum(
        "stc,cd->std",
        adapted_own,
        attention_weight[:, 3 * CA :],
        preferred_element_type=jnp.float32,
    )
    gated = (jax.nn.sigmoid(gate_part) * attended).astype(jnp.bfloat16)
    projected_out = jnp.einsum(
        "stc,cd->std", gated, output_weight, preferred_element_type=jnp.float32
    )
    out_gate = jax.nn.sigmoid(
        jnp.einsum("stc,cd->std", cond_own, output_gate_weight, preferred_element_type=jnp.float32)
    )
    attn_update = (out_gate * projected_out).astype(jnp.bfloat16)
    return (new_tile, attn_update)


def solution(mesh):
    return jax.shard_map(
        local,
        mesh=mesh,
        in_specs=(
            P("row", "col", None),
            P(),
            P(),
            P(),
            P("smp", None, None),
            P("smp"),
            P(),
            P(),
            P(),
            P(),
            P(),
            P(),
            P(),
        ),
        out_specs=(P("row", "col", None), P("smp", ("row", "col"), None)),
        check_vma=False,
    )
```

profile of v0, /device:TPU:1, one launch (start us, length us, event | category | flops | bytes accessed | tf_op | source)
XLA Modules:
  0.0 460.5 jit_solution(10458823537242216250)
XLA Ops:
  7.2 2.0 convert_reduce_fusion.1
  9.2 2.3 fusion.21
  11.6 1.7 convolution_bitcast_fusion.1
  13.5 12.3 %all_gather.21 = f32[4,32,512]{2,1,0:T(8,128)S(1)} all-gather(f32[4,32,128]{2,1,0:T(8,128)S(1)} %copy.113), channel_id=1, replica_groups=mesh['row'=4,'col'=16,'smp'=2] {'row'}, dimensions={2}, use_global_device_ids=true | all-gather | bytes 327680 | tf_op jit(solution)/shard_map/all_gather | solution.py:142
  28.1 3.8 all-to-all-start
  42.2 2.8 fusion.43
  45.0 1.7 copy.111
  53.0 2.0 fusion.78
  55.0 30.4 %all-gather.5.cloned.1.call-done = f32[4,512,512]{2,0,1:T(4,128)} async-done(((f32[4,32,512]{2,0,1:T(4,128)}), f32[4,512,512]{2,0,1:T(4,128)}) %all-gather.5.cloned.1.call-update) | async-done | bytes 4194320 | tf_op jit(solution)/shard_map/all_gather | solution.py:143
  85.4 5.2 %copy.119 = f32[4,512,512]{1,2,0:T(8,128)} copy(f32[4,512,512]{2,0,1:T(4,128)} %all-gather.5.cloned.1.call-done) | data formatting | bytes 8388608 | tf_op jit(solution)/shard_map/while | solution.py:95
  90.7 87.0 %while.29 = (s32[]{:T(128)}, bf16[8,512,128]{1,2,0:T(8,128)(2,1)}, s32[8]{0:T(128)S(1)}, f32[512,8,128]{2,0,1:T(8,128)}, bf16[512,8,128]{2,0,1:T(8,128)(2,1)}, /...) while((s32[]{:T(128)}, bf16[8,512,128]{1,2,0:T(8,128)(2,1)}, ...), condition=%wide.region_7.8_spmd, body=%wide.region_4.7_spmd.sunk | while | flops 140898304 | bytes 20750516 | solution.py:95
  96.6 3.0 fusion.174
  107.4 3.0 fusion.174
  118.3 3.0 fusion.174
  129.2 3.0 fusion.174
  140.1 3.0 fusion.174
  150.9 3.0 fusion.174
  161.8 3.0 fusion.174
  172.7 3.0 fusion.174
  177.7 1.7 fusion.26
  181.1 4.1 all-to-all-start.1
  187.3 2.6 fusion.32
  190.8 2.9 multiply_convert_fusion.2
  195.3 4.6 all-to-all-done.1
  203.2 2.9 convolution_bitcast_fusion
  208.0 1.7 copy.133
  211.0 24.7 %all-gather = f32[64,16,128]{2,1,0:T(8,128)S(1)} all-gather(f32[4,16,128]{2,1,0:T(8,128)S(1)} %get-tuple-element.335), channel_id=2, replica_groups=mesh['row'=4,'col'=16,'smp'=2] {'col'}, dimensions={0}, use_global_device_ids=true | all-gather | bytes 557056 | tf_op jit(solution)/shard_map/all_gather | solution.py:21
  236.0 22.1 %all-gather.1 = f32[64,16,128]{2,1,0:T(8,128)S(1)} all-gather(f32[4,16,128]{2,1,0:T(8,128)S(1)} %fusion.85), channel_id=3, replica_groups=mesh['row'=4,'col'=16,'smp'=2] {'col'}, dimensions={0}, use_global_device_ids=true | all-gather | bytes 557056 | tf_op jit(solution)/shard_map/all_gather | solution.py:21
  258.1 98.4 %all-gather.7.cloned.1.call-done = f32[16,4,128,768]{3,2,1,0:T(8,128)} async-done(((f32[1,4,128,768]{3,2,1,0:T(8,128)}), f32[16,4,128,768]{3,2,1,0:T(8,128)}) %all-gather.7.cloned.1.call-update) | async-done | bytes 25165840 | tf_op jit(solution)/shard_map/all_gather | solution.py:21
  358.0 1.7 copy.134
  359.7 88.7 %while.30 = (s32[]{:T(128)}, f32[4,16,128]{2,1,0:T(8,128)S(1)}, f32[4,16,128]{2,1,0:T(8,128)S(1)}, f32[4,128,768]{1,2,0:T(8,128)}, f32[16,4,16,128]{3,2,1,0:T(8,...) while((s32[]{:T(128)}, f32[4,16,128]{2,1,0:T(8,128)S(1)}, ...), condition=%wide.region_21.22_spmd, body=%wide.region_20.21_spmd.sunk | while | flops 1236997 | bytes 19890436 | solution.py:26
  362.7 2.9 fusion.179
  368.7 2.9 fusion.179
  374.6 2.9 fusion.179
  380.5 2.9 fusion.179
  386.4 2.9 fusion.179
  392.3 2.9 fusion.179
  398.2 2.9 fusion.179
  404.1 2.9 fusion.179
  410.0 2.9 fusion.179
  415.9 2.9 fusion.179
  421.9 2.9 fusion.179
  427.8 2.9 fusion.179
  433.7 2.9 fusion.179
  439.6 2.9 fusion.179
  445.5 2.9 fusion.179
  448.9 2.0 copy.136
  450.8 2.9 fusion.68
  (384 shorter events, 125.9 us)
Async XLA Ops:
  7.2 33.0 %copy-start = (bf16[384,1536]{1,0:T(8,128)(2,1)S(1)}, bf16[384,1536]{1,0:T(8,128)(2,1)}, u32[]{:S(2)}) copy-start(bf16[384,1536]{1,0:T(8,128)(2,1)} %param.25) | copy-start | bytes 3538948
  7.2 4.4 copy-start.2
  7.2 4.4 copy-start.17
  7.2 78.2 %all-gather.5.cloned.1.call-start = ((), (), s32[]{:S(2)}) async-start(), calls=%async_computation.2 | async-start | bytes 4456448 | tf_op jit(solution)/shard_map/all_gather | solution.py:143
  26.7 5.3 %copy-start.13 = (bf16[128,512]{1,0:T(8,128)(2,1)S(1)}, bf16[128,512]{1,0:T(8,128)(2,1)}, u32[]{:S(2)}) copy-start(bf16[128,512]{1,0:T(8,128)(2,1)} %param.18) | copy-start | bytes 393220
  28.1 7.4 %copy-start.18 = (s32[4]{0:T(128)S(1)}, s32[4]{0:T(128)}, u32[]{:S(2)}) copy-start(s32[4]{0:T(128)} %param.22) | copy-start | bytes 52
  28.1 7.6 %copy-start.12 = (bf16[256,384]{1,0:T(8,128)(2,1)S(1)}, bf16[256,384]{1,0:T(8,128)(2,1)}, u32[]{:S(2)}) copy-start(bf16[256,384]{1,0:T(8,128)(2,1)} %param.24) | copy-start | bytes 589828
  28.1 16.9 %all-to-all-start = ((bf16[128,32,128]{2,0,1:T(8,128)(2,1)}), bf16[128,32,128]{2,0,1:T(8,128)(2,1)S(1)}, u32[]{:S(2)}, u32[]{:S(2)}) async-start(bf16[128,32,128]{2,0,1:T(8,128)(2,1)} %copy.110), calls=%async_computation | async-start | bytes 2097152 | tf_op jit(solution)/shard_map/all_to_all | solution.py:144
  33.1 7.5 %copy-start.11 = (bf16[768,3072]{1,0:T(8,128)(2,1)S(1)}, bf16[768,3072]{1,0:T(8,128)(2,1)}, u32[]{:S(2)}) copy-start(bf16[768,3072]{1,0:T(8,128)(2,1)} %param.26) | copy-start | bytes 14155780
  90.7 87.0 %copy-start.3 = (f32[128,4,8,128]{3,0,1,2:T(8,128)S(1)}, f32[128,4,8,128]{3,0,1,2:T(8,128)}, u32[]{:S(2)}) copy-start(f32[128,4,8,128]{3,0,1,2:T(8,128)} %copy.111) | copy-start | bytes 6291460
  90.7 87.0 %copy-start.14 = (bf16[128,128]{1,0:T(8,128)(2,1)S(1)}, bf16[128,128]{1,0:T(8,128)(2,1)}, u32[]{:S(2)}) copy-start(bf16[128,128]{1,0:T(8,128)(2,1)} %param.20) | copy-start | bytes 98308
  181.1 18.8 %all-to-all-start.1 = ((bf16[512,8,128]{2,1,0:T(8,128)(2,1)}), bf16[512,8,128]{2,1,0:T(8,128)(2,1)S(1)}, u32[]{:S(2)}, u32[]{:S(2)}) async-start(bf16[512,8,128]{2,1,0:T(8,128)(2,1)} %copy.121), calls=%async_computation.1 | async-start | bytes 2097152 | tf_op jit(solution)/shard_map/all_to_all | solution.py:146
  185.2 171.3 %all-gather.7.cloned.1.call-start = ((), (), s32[]{:S(2)}) async-start(), calls=%async_computation.3 | async-start | bytes 26738688 | tf_op jit(solution)/shard_map/all_gather | solution.py:21
  199.9 3.3 copy-start.16
  206.5 1.0 copy-start.4
  209.8 1.1 copy-start.15
  362.7 2.9 copy-start.6
  362.7 2.9 copy-start.9
  365.7 1.0 copy-start.8
  368.6 2.9 copy-start.6
  368.6 2.9 copy-start.9
  374.5 2.9 copy-start.6
  374.6 2.9 copy-start.9
  380.5 2.9 copy-start.6
  380.5 2.9 copy-start.9
  386.4 2.9 copy-start.6
  386.4 2.9 copy-start.9
  392.3 2.9 copy-start.6
  392.3 2.9 copy-start.9
  398.2 2.9 copy-start.6
  398.2 2.9 copy-start.9
  404.1 2.9 copy-start.6
  404.1 2.9 copy-start.9
  410.0 2.9 copy-start.6
  410.0 2.9 copy-start.9
  415.9 2.9 copy-start.6
  415.9 2.9 copy-start.9
  421.8 2.9 copy-start.6
  421.8 2.9 copy-start.9
  427.8 2.9 copy-start.6
  427.8 2.9 copy-start.9
  433.7 2.9 copy-start.6
  433.7 2.9 copy-start.9
  439.6 2.9 copy-start.6
  439.6 2.9 copy-start.9
  445.5 2.9 copy-start.6
  445.5 2.9 copy-start.9
  448.9 4.9 %copy-start.1 = (bf16[384,1536]{1,0:T(8,128)(2,1)S(1)}, bf16[384,1536]{1,0:T(8,128)(2,1)}, u32[]{:S(2)}) copy-start(bf16[384,1536]{1,0:T(8,128)(2,1)} %param.25) | copy-start | bytes 3538948
  (31 other events, 27.5 us)
Sparse Core Ops, SparseCore 0:
  26.8 58.5 all-gather.4
  209.9 146.5 all-gather.6
where the time goes:
time: 463 us; the launch traced here: 461 us
  waiting for transfers between devices  134 us (29%)
  local copies, waits for them, and re-layouts  103 us (22%)
  other arithmetic  77.4 us (17%)
  blocking collectives  59.1 us (13%)
  matrix products  49.2 us (11%)
  loops' own time  16.2 us (3%)
  between operations  14.5 us (3%)
  starting transfers between devices  8.01 us (2%)
    all_gather x1, waiting for transfers between devices, combined_all(): gathered = jax.tree.map(lambda a: lax.all_gather(a, axis), part)  98.4 us
    all_gather x2, blocking collectives, combined_all(): gathered = jax.tree.map(lambda a: lax.all_gather(a, axis), part)  46.8 us
    add x15, other arithmetic, combine_parts(): rescale(sum_one, factor_one) + rescale(sum_two, factor_two)  43.6 us
    all_gather x1, waiting for transfers between devices, local(): bias_full = lax.all_gather(partial_bias, 'col', axis=1, tiled=True)  30.4 us
    dynamic_slice x32, local copies, waits for them, and re-layouts, take(): lax.dynamic_index_in_dim(a, source, 0, False)  29.8 us
    dot_general x8, matrix products, one_column(): jnp.einsum('ihd,khd->hik', query_col, key_col, preferred_element_type=jnp...  23.6 us
    another operation x1, loops' own time, attend_columns(): gated = lax.map(one_column, jnp.arange(col_count, dtype=jnp.int32))  15.3 us
    while x135, local copies, waits for them, and re-layouts  13.6 us
  transfers between devices with their start and end apart: 4, of which 3 were waited for; matrix products, arithmetic and copies ran while one was open for 7% of the time, Pallas kernels for 0%

commit v1 on v0

--- a/solution.py
+++ b/solution.py
@@ -140,7 +140,14 @@
         "kiz,zh->hik", normed_tile, tri_bias_weight, preferred_element_type=jnp.float32
     )
     partial_bias = lax.all_gather(local_bias, "row", axis=2, tiled=True)
-    bias_full = lax.all_gather(partial_bias, "col", axis=1, tiled=True)
+
+    def hold_levels_all(z_in):
+        y_new = lax.psum(1, "col")
+        k_now = jnp.stack(y_new * [z_in])
+        part_now = lax.all_to_all(k_now, "col", 0, 0)
+        return jnp.concatenate(part_now, axis=1)
+
+    bias_full = hold_levels_all(partial_bias)
     columns = lax.all_to_all(pair_repr, "row", split_axis=1, concat_axis=0, tiled=True)
     updated = attend_columns(columns, bias_full, tri_weight, tri_output_weight)
     new_tile = lax.all_to_all(updated, "row", split_axis=0, concat_axis=1, tiled=True)

time: 463 us -> 503 us (1.086)
  starting transfers between devices: 8.01 us -> 20.3 us
  local copies, waits for them, and re-layouts: 103 us -> 112 us
  blocking collectives: 59.1 us -> 66.8 us
  waiting for transfers between devices: 134 us -> 141 us
    all_to_all x0 -> x1, waiting for transfers between devices: none -> 37.3 us  [hold_levels_all(): part_now = lax.all_to_all(k_now, 'col', 0, 0)]
    all_gather x1 -> x0, waiting for transfers between devices: 30.4 us -> none  [local(): bias_full = lax.all_gather(partial_bias, 'col', axis=1, tiled=True)]
    all_to_all x0 -> x1, starting transfers between devices: none -> 10.5 us  [hold_levels_all(): part_now = lax.all_to_all(k_now, 'col', 0, 0)]
    all_gather x2, blocking collectives: 46.8 us -> 56.3 us  [combined_all(): gathered = jax.tree.map(lambda a: lax.all_gather(a, axis), part)]
  transfers between devices with their start and end apart: 4 -> 4, of which waited for: 3 -> 3; matrix products, arithmetic and copies ran while one was open for 7% -> 9% of each run, Pallas kernels for 0% -> 0%
where the time goes in v1:
time: 503 us; the launch traced here: 500 us
  waiting for transfers between devices  141 us (28%)
  local copies, waits for them, and re-layouts  112 us (22%)
  other arithmetic  76.7 us (15%)
  blocking collectives  66.8 us (13%)
  matrix products  51.9 us (10%)
  starting transfers between devices  20.3 us (4%)
  loops' own time  17 us (3%)
  between operations  14.5 us (3%)
    all_gather x1, waiting for transfers between devices, combined_all(): gathered = jax.tree.map(lambda a: lax.all_gather(a, axis), part)  98.8 us
    all_gather x2, blocking collectives, combined_all(): gathered = jax.tree.map(lambda a: lax.all_gather(a, axis), part)  56.3 us
    add x15, other arithmetic, combine_parts(): rescale(sum_one, factor_one) + rescale(sum_two, factor_two)  43.6 us
    all_to_all x1, waiting for transfers between devices, hold_levels_all(): part_now = lax.all_to_all(k_now, 'col', 0, 0)  37.3 us
    dynamic_slice x32, local copies, waits for them, and re-layouts, take(): lax.dynamic_index_in_dim(a, source, 0, False)  29.8 us
    dot_general x8, matrix products, one_column(): jnp.einsum('ihd,khd->hik', query_col, key_col, preferred_element_type=jnp...  23.6 us
    another operation x1, loops' own time, attend_columns(): gated = lax.map(one_column, jnp.arange(col_count, dtype=jnp.int32))  16 us
    while x135, local copies, waits for them, and re-layouts  13.6 us
  transfers between devices with their start and end apart: 4, of which 3 were waited for; matrix products, arithmetic and copies ran while one was open for 9% of the time, Pallas kernels for 0%

profile of v1, /device:TPU:1, one launch (start us, length us, event | category | flops | bytes accessed | tf_op | source)
XLA Modules:
  0.0 500.3 jit_solution(797168059240024389)
XLA Ops:
  7.2 2.8 copy.116
  9.9 6.0 %all-to-all-start = ((bf16[128,32,128]{2,0,1:T(8,128)(2,1)}), bf16[128,32,128]{2,0,1:T(8,128)(2,1)S(1)}, u32[]{:S(2)}, u32[]{:S(2)}) async-start(bf16[128,32,128]{2,0,1:T(8,128)(2,1)} %copy.116), calls=%async_computation | async-start | bytes 2097152 | tf_op jit(solution)/shard_map/all_to_all | solution.py:151
  26.4 2.6 convolution_bitcast_fusion.1
  32.2 10.5 %all_gather.18 = f32[4,32,512]{2,1,0:T(8,128)S(1)} all-gather(f32[4,32,128]{2,1,0:T(8,128)S(1)} %copy.119), channel_id=1, replica_groups=mesh['row'=4,'col'=16,'smp'=2] {'row'}, dimensions={2}, use_global_device_ids=true | all-gather | bytes 327680 | tf_op jit(solution)/shard_map/all_gather | solution.py:142
  42.9 2.5 stack.2
  45.4 10.5 %all-to-all-start.1 = ((f32[16,4,32,512]{3,2,1,0:T(8,128)}), f32[16,4,32,512]{3,2,1,0:T(8,128)}, u32[]{:S(2)}, u32[]{:S(2)}) async-start(f32[16,4,32,512]{3,2,1,0:T(8,128)} %stack.2), calls=%async_computation.1 | async-start | bytes 8388608 | tf_op jit(solution)/shard_map/all_to_all | solution.py:147
  57.9 2.4 convolution_convert_fusion
  61.1 2.8 fusion.43
  71.9 2.0 fusion.78
  73.9 37.3 %all-to-all-done.1 = f32[16,4,32,512]{3,2,1,0:T(8,128)} async-done(((f32[16,4,32,512]{3,2,1,0:T(8,128)}), f32[16,4,32,512]{3,2,1,0:T(8,128)}, u32[]{:S(2)}, u32[]{:S(2)}) %all-to-all-start.1) | async-done | bytes 4194336 | tf_op jit(solution)/shard_map/all_to_all | solution.py:147
  111.3 5.0 copy.120
  116.2 5.2 %copy.125 = f32[4,512,512]{1,2,0:T(8,128)} copy(f32[4,512,512]{2,1,0:T(8,128)} %bitcast.197) | data formatting | bytes 8388608 | tf_op jit(solution)/shard_map/while | solution.py:95
  121.5 87.7 %while.29 = (s32[]{:T(128)}, bf16[8,512,128]{1,2,0:T(8,128)(2,1)}, s32[8]{0:T(128)S(1)}, f32[512,8,128]{2,0,1:T(8,128)}, bf16[512,8,128]{2,0,1:T(8,128)(2,1)}, /...) while((s32[]{:T(128)}, bf16[8,512,128]{1,2,0:T(8,128)(2,1)}, ...), condition=%wide.region_7.8_spmd, body=%wide.region_4.7_spmd.sunk | while | flops 140898304 | bytes 20750516 | solution.py:95
  127.4 3.0 fusion.174
  138.4 3.0 fusion.174
  149.4 3.0 fusion.174
  160.3 3.0 fusion.174
  171.3 3.0 fusion.174
  182.2 3.0 fusion.174
  193.2 3.0 fusion.174
  204.1 3.0 fusion.174
  212.5 3.6 all-to-all-start.2
  217.6 2.6 fusion.32
  221.1 2.9 multiply_convert_fusion.2
  225.6 4.8 all-to-all-done.2
  233.7 2.9 convolution_bitcast_fusion
  237.9 1.7 copy.139
  240.9 35.4 %all-gather = f32[64,16,128]{2,1,0:T(8,128)S(1)} all-gather(f32[4,16,128]{2,1,0:T(8,128)S(1)} %get-tuple-element.335), channel_id=2, replica_groups=mesh['row'=4,'col'=16,'smp'=2] {'col'}, dimensions={0}, use_global_device_ids=true | all-gather | bytes 557056 | tf_op jit(solution)/shard_map/all_gather | solution.py:21
  276.6 20.9 %all-gather.1 = f32[64,16,128]{2,1,0:T(8,128)S(1)} all-gather(f32[4,16,128]{2,1,0:T(8,128)S(1)} %fusion.85), channel_id=3, replica_groups=mesh['row'=4,'col'=16,'smp'=2] {'col'}, dimensions={0}, use_global_device_ids=true | all-gather | bytes 557056 | tf_op jit(solution)/shard_map/all_gather | solution.py:21
  297.5 98.8 %all-gather.4.cloned.1.call-done = f32[16,4,128,768]{3,2,1,0:T(8,128)} async-done(((f32[1,4,128,768]{3,2,1,0:T(8,128)}), f32[16,4,128,768]{3,2,1,0:T(8,128)}) %all-gather.4.cloned.1.call-update) | async-done | bytes 25165840 | tf_op jit(solution)/shard_map/all_gather | solution.py:21
  399.5 88.7 %while.30 = (s32[]{:T(128)}, f32[4,16,128]{2,1,0:T(8,128)S(1)}, f32[4,16,128]{2,1,0:T(8,128)S(1)}, f32[4,128,768]{1,2,0:T(8,128)}, f32[16,4,16,128]{3,2,1,0:T(8,...) while((s32[]{:T(128)}, f32[4,16,128]{2,1,0:T(8,128)S(1)}, ...), condition=%wide.region_21.22_spmd, body=%wide.region_20.21_spmd.sunk | while | flops 1236997 | bytes 19890436 | solution.py:26
  402.5 2.9 fusion.179
  408.5 2.9 fusion.179
  414.4 2.9 fusion.179
  420.3 2.9 fusion.179
  426.2 2.9 fusion.179
  432.1 2.9 fusion.179
  438.0 2.9 fusion.179
  443.9 2.9 fusion.179
  449.8 2.9 fusion.179
  455.7 2.9 fusion.179
  461.7 2.9 fusion.179
  467.6 2.9 fusion.179
  473.5 2.9 fusion.179
  479.4 2.9 fusion.179
  485.3 2.9 fusion.179
  488.7 2.0 copy.142
  490.6 2.9 fusion.68
  (384 shorter events, 133.5 us)
Async XLA Ops:
  7.2 50.3 %copy-start = (bf16[384,1536]{1,0:T(8,128)(2,1)S(1)}, bf16[384,1536]{1,0:T(8,128)(2,1)}, u32[]{:S(2)}) copy-start(bf16[384,1536]{1,0:T(8,128)(2,1)} %param.25) | copy-start | bytes 3538948
  7.2 8.8 %copy-start.2 = (bf16[128,32,128]{2,1,0:T(8,128)(2,1)S(1)}, bf16[128,32,128]{2,1,0:T(8,128)(2,1)}, u32[]{:S(2)}) copy-start(bf16[128,32,128]{2,1,0:T(8,128)(2,1)} %param.17) | copy-start | bytes 3145732
  9.9 11.3 %copy-start.18 = (s32[4]{0:T(128)S(1)}, s32[4]{0:T(128)}, u32[]{:S(2)}) copy-start(s32[4]{0:T(128)} %param.22) | copy-start | bytes 52
  9.9 33.0 %all-to-all-start = ((bf16[128,32,128]{2,0,1:T(8,128)(2,1)}), bf16[128,32,128]{2,0,1:T(8,128)(2,1)S(1)}, u32[]{:S(2)}, u32[]{:S(2)}) async-start(bf16[128,32,128]{2,0,1:T(8,128)(2,1)} %copy.116), calls=%async_computation | async-start | bytes 2097152 | tf_op jit(solution)/shard_map/all_to_all | solution.py:151
  15.9 10.5 %copy-start.17 = (bf16[128,4]{0,1:T(4,128)(2,1)S(1)}, bf16[128,4]{0,1:T(4,128)(2,1)}, u32[]{:S(2)}) copy-start(bf16[128,4]{0,1:T(4,128)(2,1)} %param.19) | copy-start | bytes 3076
  45.4 65.8 %all-to-all-start.1 = ((f32[16,4,32,512]{3,2,1,0:T(8,128)}), f32[16,4,32,512]{3,2,1,0:T(8,128)}, u32[]{:S(2)}, u32[]{:S(2)}) async-start(f32[16,4,32,512]{3,2,1,0:T(8,128)} %stack.2), calls=%async_computation.1 | async-start | bytes 8388608 | tf_op jit(solution)/shard_map/all_to_all | solution.py:147
  55.9 1.9 copy-start.14
  66.4 2.6 copy-start.12
  121.5 87.7 %copy-start.3 = (f32[128,4,8,128]{3,0,1,2:T(8,128)S(1)}, f32[128,4,8,128]{3,0,1,2:T(8,128)}, u32[]{:S(2)}) copy-start(f32[128,4,8,128]{3,0,1,2:T(8,128)} %copy.117) | copy-start | bytes 6291460
  121.5 87.7 %copy-start.13 = (bf16[128,128]{1,0:T(8,128)(2,1)S(1)}, bf16[128,128]{1,0:T(8,128)(2,1)}, u32[]{:S(2)}) copy-start(bf16[128,128]{1,0:T(8,128)(2,1)} %param.20) | copy-start | bytes 98308
  210.8 5.5 %copy-start.11 = (bf16[4,32,768]{2,1,0:T(8,128)(2,1)S(1)}, bf16[4,32,768]{2,1,0:T(8,128)(2,1)}, u32[]{:S(2)}) copy-start(bf16[4,32,768]{2,1,0:T(8,128)(2,1)} %get-tuple-element.327) | copy-start | bytes 589828
  210.9 6.1 %copy-start.10 = (bf16[4,32,768]{2,1,0:T(8,128)(2,1)S(1)}, bf16[4,32,768]{2,1,0:T(8,128)(2,1)}, u32[]{:S(2)}) copy-start(bf16[4,32,768]{2,1,0:T(8,128)(2,1)} %get-tuple-element.328) | copy-start | bytes 589828
  212.5 17.8 %all-to-all-start.2 = ((bf16[512,8,128]{2,1,0:T(8,128)(2,1)}), bf16[512,8,128]{2,1,0:T(8,128)(2,1)S(1)}, u32[]{:S(2)}, u32[]{:S(2)}) async-start(bf16[512,8,128]{2,1,0:T(8,128)(2,1)} %copy.127), calls=%async_computation.2 | async-start | bytes 2097152 | tf_op jit(solution)/shard_map/all_to_all | solution.py:153
  216.1 180.2 %all-gather.4.cloned.1.call-start = ((), (), s32[]{:S(2)}) async-start(), calls=%async_computation.3 | async-start | bytes 26738688 | tf_op jit(solution)/shard_map/all_gather | solution.py:21
  230.4 3.3 copy-start.16
  239.6 1.1 copy-start.15
  402.5 2.9 copy-start.5
  402.5 2.9 copy-start.8
  405.5 1.0 copy-start.7
  408.4 2.9 copy-start.5
  408.4 2.9 copy-start.8
  414.3 2.9 copy-start.5
  414.4 2.9 copy-start.8
  420.3 2.9 copy-start.5
  420.3 2.9 copy-start.8
  426.2 2.9 copy-start.5
  426.2 2.9 copy-start.8
  432.1 2.9 copy-start.5
  432.1 2.9 copy-start.8
  438.0 2.9 copy-start.5
  438.0 2.9 copy-start.8
  443.9 2.9 copy-start.5
  443.9 2.9 copy-start.8
  449.8 2.9 copy-start.5
  449.8 2.9 copy-start.8
  455.7 2.9 copy-start.5
  455.7 2.9 copy-start.8
  461.6 2.9 copy-start.5
  461.6 2.9 copy-start.8
  467.5 2.9 copy-start.5
  467.6 2.9 copy-start.8
  473.5 2.9 copy-start.5
  473.5 2.9 copy-start.8
  479.4 2.9 copy-start.5
  479.4 2.9 copy-start.8
  485.3 2.9 copy-start.5
  485.3 2.9 copy-start.8
  488.6 4.9 copy-start.1
  (31 other events, 27.5 us)
Sparse Core Ops, SparseCore 0:
  239.8 156.4 all-gather.3
